TPU v7x, 32 devices: a whole 2x2x4 slice. The times are simulated.
32 devices in a mesh: grp: 4 (over x, core), ep: 8 (over z, y).
Axes of the slice: x: 2, y: 2, z: 4, core: 2. Of those that a mesh axis runs over, the one named last changes fastest.
Arguments:
- tokens: bfloat16 [32768, 512], P(('grp', 'ep')), may hold values from -6 to 6
- segments: int32 [128, 256], P(('grp', 'ep')), may hold values from 0 to 7, never falling along the last dimension, each value on 1 to 128 neighbouring positions
- patch_mask: int32 [128, 256], P(('grp', 'ep')), may hold values 0 or 1
- choices: int32 [32768, 2], P(('grp', 'ep')), may hold values from 0 to 7, all different within a row
- priority: int32 [32, 1024], P(('grp', 'ep')), may hold values from 0 to 1023, each once within a row
- first_gain: bfloat16 [512], P(('grp', 'ep')), may hold values from 0.5 to 1.5
- joint_weight: bfloat16 [512, 1536], P(('grp', 'ep')), may hold values from -0.25 to 0.25
- output_weight: bfloat16 [512, 512], P(('grp', 'ep')), may hold values from -1 to 1
- second_gain: bfloat16 [512], P(('grp', 'ep')), may hold values from 0.5 to 1.5
- router_weight: bfloat16 [512, 8], P(('grp', 'ep')), may hold values from -0.19921875 to 0.19921875
- expert_up: bfloat16 [8, 512, 2048], P('ep'), may hold values from -0.25 to 0.25
- expert_down: bfloat16 [8, 2048, 512], P('ep'), may hold values from -0.75 to 0.75
- out_grad: bfloat16 [32768, 512], P(('grp', 'ep')), may hold values from -6 to 6
Outputs:
- output: bfloat16 [32768, 512], P(('grp', 'ep'))
- tokens_grad: float32 [32768, 512], P(('grp', 'ep'))
- first_gain_grad: float32 [512], P(('grp', 'ep'))
- joint_weight_grad: float32 [512, 1536], P(('grp', 'ep'))
- output_weight_grad: float32 [512, 512], P(('grp', 'ep'))
- second_gain_grad: float32 [512], P(('grp', 'ep'))
- router_weight_grad: float32 [512, 8], P(('grp', 'ep'))
- expert_up_grad: float32 [8, 512, 2048], P('ep')
- expert_down_grad: float32 [8, 2048, 512], P('ep')
Inputs may be any that keep to these rules, and one draw needn't show every extreme that they name: `segments`: within a sequence the ids never fall. `choices`: a token's two experts differ. `priority`: each row holds every number below 1024 once.
All inputs are finite; a program needn't handle non-finite values. No bound on the sum of `patch_mask` on one device may be relied on, other than what follows from the above.
Results may differ from a plain program's by a relative error of at most 0.013.
Values may be sent and summed in bfloat16 or wider, within the bound.
A program may use at most 192 MiB of HBM per device.

v0:
```python
import jax
import jax.numpy as jnp
from jax import lax
from jax.sharding import PartitionSpec as P

HEADS = 8
EPSILON = 1e-06
NEGATIVE = -1e30


def normalize(values, gain):
    mean = jnp.mean(values, axis=-1, keepdims=True)
    centred = values - mean
    inverse = lax.rsqrt(jnp.mean(centred * centred, axis=-1, keepdims=True) + EPSILON)
    unit = centred * inverse
    return (unit * gain, unit, inverse)


def normalize_back(incoming, gain, unit, inverse):
    scaled = incoming * gain
    inner = (
        scaled
        - jnp.mean(scaled, axis=-1, keepdims=True)
        - unit * jnp.mean(scaled * unit, axis=-1, keepdims=True)
    )
    return (inverse * inner, jnp.sum(incoming * unit, axis=0))


def outer(left, right):
    return lax.dot_general(
        left, right, (((0,), (0,)), ((), ())), preferred_element_type=jnp.float32
    )


def times_t(left, right):
    return lax.dot_general(
        left, right, (((1,), (1,)), ((), ())), preferred_element_type=jnp.float32
    )


def gelu_slope(values):
    normal_cdf = 0.5 * (1.0 + lax.erf(values * 0.7071067811865476))
    density = jnp.exp(-0.5 * values * values) * 0.3989422804014327
    return normal_cdf + values * density


def route(picks, live, ranks, expert_count, capacity):
    row_count = picks.shape[0]
    labels = lax.broadcasted_iota(jnp.int32, (row_count, expert_count), 1)
    first = (picks[:, 0:1] == labels).astype(jnp.int32)
    second = (picks[:, 1:2] == labels).astype(jnp.int32)
    live_col = live[:, None]
    earlier = (ranks[None, :] < ranks[:, None]).astype(jnp.int32)
    first_live = first * live_col
    second_live = second * live_col
    place_one = jnp.sum(
        jnp.dot(earlier, first_live, preferred_element_type=jnp.int32) * first, axis=1
    )
    ahead = (
        jnp.dot(earlier, second_live, preferred_element_type=jnp.int32)
        + jnp.sum(first_live, axis=0)[None, :]
    )
    place_two = jnp.sum(ahead * second, axis=1)
    keep_one = (live > 0) & (place_one < capacity)
    keep_two = (live > 0) & (place_two < capacity)
    dummy = expert_count * capacity
    slot_one = jnp.where(keep_one, picks[:, 0] * capacity + place_one, dummy)
    slot_two = jnp.where(keep_two, picks[:, 1] * capacity + place_two, dummy)
    pick_one = (first * keep_one[:, None].astype(jnp.int32)).astype(jnp.float32)
    pick_two = (second * keep_two[:, None].astype(jnp.int32)).astype(jnp.float32)
    return (slot_one, slot_two, pick_one, pick_two)


def visible(group, live):
    rows = group.shape[0]
    index = lax.broadcasted_iota(jnp.int32, (rows, rows), 0)
    other = lax.broadcasted_iota(jnp.int32, (rows, rows), 1)
    return (group[:, None] == group[None, :]) & ((live[None, :] > 0) | (index == other))


def attend_forward(query, key, value, allowed, factor):
    scores = jnp.einsum("qhd,khd->hqk", query, key, preferred_element_type=jnp.float32) * factor
    masked = jnp.where(allowed[None], scores, NEGATIVE)
    top = jnp.max(masked, axis=-1, keepdims=True)
    weights = jnp.exp(masked - top)
    total = jnp.sum(weights, axis=-1, keepdims=True)
    probs = (weights / total).astype(jnp.bfloat16)
    mixed = jnp.einsum("hqk,khd->qhd", probs, value, preferred_element_type=jnp.float32)
    return (mixed, top + jnp.log(total))


def attend_backward(query, key, value, allowed, log_total, grad_mixed, factor):
    scores = jnp.einsum("qhd,khd->hqk", query, key, preferred_element_type=jnp.float32) * factor
    masked = jnp.where(allowed[None], scores, NEGATIVE)
    probs = jnp.exp(masked - log_total)
    grad_value = jnp.einsum(
        "hqk,qhd->khd", probs.astype(jnp.bfloat16), grad_mixed, preferred_element_type=jnp.float32
    )
    grad_probs = jnp.einsum("qhd,khd->hqk", grad_mixed, value, preferred_element_type=jnp.float32)
    delta = jnp.sum(probs * grad_probs, axis=-1, keepdims=True)
    grad_scores = (probs * (grad_probs - delta)).astype(jnp.bfloat16)
    grad_query = (
        jnp.einsum("hqk,khd->qhd", grad_scores, key, preferred_element_type=jnp.float32) * factor
    )
    grad_key = (
        jnp.einsum("hqk,qhd->khd", grad_scores, query, preferred_element_type=jnp.float32) * factor
    )
    return jnp.stack([grad_query, grad_key, grad_value], axis=1)


def per_device(
    tokens,
    segments,
    patch_mask,
    choices,
    priority,
    first_gain,
    joint_weight,
    output_weight,
    second_gain,
    router_weight,
    expert_up,
    expert_down,
    out_grad,
):
    row_count, width = tokens.shape
    head_size = width // HEADS
    factor = head_size ** (-0.5)
    expert_count = router_weight.shape[1]
    length = segments.shape[1]
    capacity = (21 * choices.shape[1] * row_count + 20 * expert_count - 1) // (20 * expert_count)
    block_rows = min(row_count, 512)
    gain_one, joint_full, output_full, gain_two, router_full = (
        lax.all_gather(first_gain, ("grp", "ep"), axis=0, tiled=True),
        lax.all_gather(joint_weight, ("grp", "ep"), axis=0, tiled=True),
        lax.all_gather(output_weight, ("grp", "ep"), axis=0, tiled=True),
        lax.all_gather(second_gain, ("grp", "ep"), axis=0, tiled=True),
        lax.all_gather(router_weight, ("grp", "ep"), axis=0, tiled=True),
    )
    inputs = tokens.astype(jnp.float32)
    gain_one = gain_one.astype(jnp.float32)
    gain_two = gain_two.astype(jnp.float32)
    normed_f, unit_one, inverse_one = normalize(inputs, gain_one)
    normed = normed_f.astype(jnp.bfloat16)
    joint = jnp.dot(normed, joint_full, preferred_element_type=jnp.float32).astype(jnp.bfloat16)
    joint = joint.reshape(row_count, 3, HEADS, head_size)
    live = patch_mask.reshape(row_count)
    position = lax.broadcasted_iota(jnp.int32, (row_count,), 0)
    group = position // length * length + segments.reshape(row_count)
    masks = []
    mixed_parts = []
    log_parts = []
    for start in range(0, row_count, block_rows):
        allowed = visible(group[start : start + block_rows], live[start : start + block_rows])
        block = joint[start : start + block_rows]
        mixed_block, log_total = attend_forward(
            block[:, 0], block[:, 1], block[:, 2], allowed, factor
        )
        masks.append(allowed)
        mixed_parts.append(mixed_block)
        log_parts.append(log_total)
    mixed = jnp.concatenate(mixed_parts, axis=0).reshape(row_count, width).astype(jnp.bfloat16)
    state = inputs + jnp.dot(mixed, output_full, preferred_element_type=jnp.float32)
    normed_two_f, unit_two, inverse_two = normalize(state, gain_two)
    normed_two = normed_two_f.astype(jnp.bfloat16)
    logits = jnp.dot(normed_two, router_full, preferred_element_type=jnp.float32)
    gate = jax.nn.softmax(logits, axis=-1)
    slot_one, slot_two, pick_one, pick_two = route(
        choices, live, priority.reshape(row_count), expert_count, capacity
    )
    gate_one = jnp.sum(gate * pick_one, axis=1)
    gate_two = jnp.sum(gate * pick_two, axis=1)
    empty = jnp.zeros((expert_count * capacity + 1, width), jnp.bfloat16)
    outgoing = empty.at[slot_one].add(normed_two).at[slot_two].add(normed_two)
    outgoing = outgoing[: expert_count * capacity].reshape(expert_count, capacity, width)
    arrived = lax.all_to_all(outgoing, "ep", split_axis=0, concat_axis=1, tiled=True)
    pre = jnp.einsum("erd,edf->erf", arrived, expert_up, preferred_element_type=jnp.float32)
    act = jax.nn.gelu(pre, approximate=False).astype(jnp.bfloat16)
    produced = jnp.einsum(
        "erf,efd->erd", act, expert_down, preferred_element_type=jnp.float32
    ).astype(jnp.bfloat16)
    returned = lax.all_to_all(produced, "ep", split_axis=1, concat_axis=0, tiled=True)
    zero_row = jnp.zeros((1, width), jnp.bfloat16)
    flat = jnp.concatenate([returned.reshape(expert_count * capacity, width), zero_row], axis=0)
    got_one = flat[slot_one].astype(jnp.float32)
    got_two = flat[slot_two].astype(jnp.float32)
    output = (state + gate_one[:, None] * got_one + gate_two[:, None] * got_two).astype(
        jnp.bfloat16
    )
    grad = out_grad.astype(jnp.float32)
    grad_gate = (
        pick_one * jnp.sum(grad * got_one, axis=1)[:, None]
        + pick_two * jnp.sum(grad * got_two, axis=1)[:, None]
    )
    grad_logits = (gate * (grad_gate - jnp.sum(gate * grad_gate, axis=1, keepdims=True))).astype(
        jnp.bfloat16
    )
    grad_router = outer(normed_two, grad_logits)
    grad_normed_two = times_t(grad_logits, router_full)
    weighted_one = (gate_one[:, None] * grad).astype(jnp.bfloat16)
    weighted_two = (gate_two[:, None] * grad).astype(jnp.bfloat16)
    grad_out_rows = empty.at[slot_one].add(weighted_one).at[slot_two].add(weighted_two)
    grad_out_rows = grad_out_rows[: expert_count * capacity].reshape(expert_count, capacity, width)
    grad_arrived = lax.all_to_all(grad_out_rows, "ep", split_axis=0, concat_axis=1, tiled=True)
    rows_now = lax.all_to_all(outgoing, "ep", split_axis=0, concat_axis=1, tiled=True)
    pre_now = jnp.einsum("erd,edf->erf", rows_now, expert_up, preferred_element_type=jnp.float32)
    act_now = jax.nn.gelu(pre_now, approximate=False).astype(jnp.bfloat16)
    grad_down = jnp.einsum(
        "erf,erd->efd", act_now, grad_arrived, preferred_element_type=jnp.float32
    )
    grad_act = jnp.einsum(
        "erd,efd->erf", grad_arrived, expert_down, preferred_element_type=jnp.float32
    )
    grad_pre = (grad_act * gelu_slope(pre_now)).astype(jnp.bfloat16)
    grad_up = jnp.einsum("erd,erf->edf", rows_now, grad_pre, preferred_element_type=jnp.float32)
    grad_rows = jnp.einsum(
        "erf,edf->erd", grad_pre, expert_up, preferred_element_type=jnp.float32
    ).astype(jnp.bfloat16)
    grad_back = lax.all_to_all(grad_rows, "ep", split_axis=1, concat_axis=0, tiled=True)
    flat_grad = jnp.concatenate(
        [grad_back.reshape(expert_count * capacity, width), zero_row], axis=0
    )
    grad_normed_two = (
        grad_normed_two
        + flat_grad[slot_one].astype(jnp.float32)
        + flat_grad[slot_two].astype(jnp.float32)
    )
    grad_state_in, grad_gain_two = normalize_back(grad_normed_two, gain_two, unit_two, inverse_two)
    grad_state = grad + grad_state_in
    grad_branch = grad_state.astype(jnp.bfloat16)
    grad_output_w = outer(mixed, grad_branch)
    grad_mixed = (
        times_t(grad_branch, output_full).astype(jnp.bfloat16).reshape(row_count, HEADS, head_size)
    )
    grad_parts = []
    for number, start in enumerate(range(0, row_count, block_rows)):
        block = joint[start : start + block_rows]
        grad_parts.append(
            attend_backward(
                block[:, 0],
                block[:, 1],
                block[:, 2],
                masks[number],
                log_parts[number],
                grad_mixed[start : start + block_rows],
                factor,
            )
        )
    grad_joint = (
        jnp.concatenate(grad_parts, axis=0).reshape(row_count, 3 * width).astype(jnp.bfloat16)
    )
    grad_joint_w = outer(normed, grad_joint)
    grad_normed = times_t(grad_joint, joint_full)
    grad_inputs_in, grad_gain_one = normalize_back(grad_normed, gain_one, unit_one, inverse_one)
    tokens_grad = grad_state + grad_inputs_in
    shares = (
        lax.psum_scatter(grad_gain_one, ("grp", "ep"), scatter_dimension=0, tiled=True),
        lax.psum_scatter(grad_joint_w, ("grp", "ep"), scatter_dimension=0, tiled=True),
        lax.psum_scatter(grad_output_w, ("grp", "ep"), scatter_dimension=0, tiled=True),
        lax.psum_scatter(grad_gain_two, ("grp", "ep"), scatter_dimension=0, tiled=True),
        lax.psum_scatter(grad_router, ("grp", "ep"), scatter_dimension=0, tiled=True),
    )
    grad_up, grad_down = (
        lax.psum(grad_up.astype(jnp.bfloat16), "grp").astype(jnp.float32),
        lax.psum(grad_down.astype(jnp.bfloat16), "grp").astype(jnp.float32),
    )
    return (
        output,
        tokens_grad,
        shares[0],
        shares[1],
        shares[2],
        shares[3],
        shares[4],
        grad_up,
        grad_down,
    )


def solution(mesh):
    in_specs = (
        P(("grp", "ep"), None),
        P(("grp", "ep"), None),
        P(("grp", "ep"), None),
        P(("grp", "ep"), None),
        P(("grp", "ep"), None),
        P(("grp", "ep")),
        P(("grp", "ep"), None),
        P(("grp", "ep"), None),
        P(("grp", "ep")),
        P(("grp", "ep"), None),
        P("ep", None, None),
        P("ep", None, None),
        P(("grp", "ep"), None),
    )
    out_specs = (
        P(("grp", "ep"), None),
        P(("grp", "ep"), None),
        P(("grp", "ep")),
        P(("grp", "ep"), None),
        P(("grp", "ep"), None),
        P(("grp", "ep")),
        P(("grp", "ep"), None),
        P("ep", None, None),
        P("ep", None, None),
    )
    return jax.shard_map(
        per_device, mesh=mesh, in_specs=in_specs, out_specs=out_specs, check_vma=False
    )
```

profile of v0, /device:TPU:0, one launch (start us, length us, event | category | flops | bytes accessed | tf_op | source)
XLA Modules:
  0.0 1114.1 jit_solution(8089762748541029859)
XLA Ops:
  11.2 42.1 %all-reduce.7 = (bf16[512]{0:T(512)(128)(2,1)S(1)}, bf16[512]{0:T(512)(128)(2,1)S(1)}) all-reduce(bf16[512]{0:T(512)(128)(2,1)S(1)} %dynamic-update-slice, bf16[512]{0:T(512)(128)(2,1)S(1)} %dynamic-update-slice.1), channel_id=1, replica_groups=mesh['grp'=4,'ep'=8] {'grp','ep'}, use_global_device_ids=true, to_apply=%add.2 | all-reduce | flops 1024 | bytes 4096
  65.6 74.1 %all_gather.17 = bf16[512,512]{1,0:T(8,128)(2,1)} all-gather(bf16[16,512]{1,0:T(8,128)(2,1)S(1)} %copy-done.51), channel_id=1, replica_groups=mesh['grp'=4,'ep'=8] {'grp','ep'}, dimensions={0}, use_global_device_ids=true | all-gather | bytes 540672 | tf_op jit(solution)/shard_map/all_gather | solution.py:136
  173.4 9.2 scatter_custom_fusion
  182.6 10.6 scatter_fusion
  200.0 53.0 %all_to_all.16 = bf16[8,269,512]{2,1,0:T(8,128)(2,1)} all-to-all(bf16[8,269,512]{2,1,0:T(8,128)(2,1)} %reshape.421), channel_id=1, replica_groups=mesh['grp'=4,'ep'=8] {'ep'}, dimensions={0} | all-to-all | bytes 4407296 | tf_op jit(solution)/shard_map/all_to_all | solution.py:176
  256.7 43.5 %fusion.2 = (bf16[2152,2048]{1,0:T(8,128)(2,1)S(1)}, f32[2152,2048]{1,0:T(8,128)}) fusion(bf16[2152,512]{1,0:T(8,128)(2,1)} %reshape.422, bf16[1,512,2048]{2,1,0:T(8,128)(2,1)S(1)} %copy-done), kind=kOutput, calls=%fused_computation.12 | convolution fusion | flops 4799545344 | bytes 30744576 | tf_op jit(solution)/shard_map/erd,edf->erf/dot_general | solution.py:177
  305.9 16.4 %copy.139 = bf16[1,2152,512]{2,0,1:T(2,128)(2,1)} copy(bf16[1,2152,512]{2,1,0:T(8,128)(2,1)S(1)} %fusion.32) | data formatting | bytes 4407296 | tf_op jit(solution)/shard_map/convert_element_type | solution.py:181
  322.8 16.5 %reduce = bf16[2152,512]{1,0:T(8,128)(2,1)} reduce(bf16[2152,1,512]{2,1,0:T(2,128)(2,1)} %bitcast.160, bf16[]{:T(256)} %broadcast.495), dimensions={1}, to_apply=%bitcast.153.reduce_sub_computation | reduce | bytes 4407298
  349.1 102.5 %all-gather = bf16[32,16,8]{1,2,0:T(8,128)(2,1)S(1)} all-gather(bf16[1,16,8]{1,2,0:T(8,128)(2,1)S(1)} %bitcast.205), channel_id=1, replica_groups=mesh['grp'=4,'ep'=8] {'grp','ep'}, dimensions={0}, use_global_device_ids=true | all-gather | bytes 8448 | tf_op jit(solution)/shard_map/all_gather | solution.py:138
  453.4 7.9 reshape.506
  492.9 9.0 scatter_custom_fusion.2
  501.9 10.6 scatter_fusion.1
  519.3 52.0 %all_to_all.17 = bf16[8,269,512]{2,1,0:T(8,128)(2,1)} all-to-all(bf16[8,269,512]{2,1,0:T(8,128)(2,1)} %reshape.426), channel_id=1, replica_groups=mesh['grp'=4,'ep'=8] {'ep'}, dimensions={0} | all-to-all | bytes 4407296 | tf_op jit(solution)/shard_map/all_to_all | solution.py:204
  574.9 13.4 %fusion.8 = bf16[2152,2048]{1,0:T(8,128)(2,1)S(1)} fusion(f32[2152,2048]{1,0:T(8,128)} %get-tuple-element.87, bf16[2152,512]{1,0:T(8,128)(2,1)} %reshape.427, bf16[1,2048,512]{2,1,0:T(8,128)(2,1)} %param.24), kind=kOutput, calls=%fused_computation.18 | convolution fusion | flops 4557144064 | bytes 30744576 | tf_op jit(solution)/shard_map/erd,efd->erf/dot_general | solution.py:211
  593.7 16.4 %copy.138 = bf16[1,2152,512]{2,0,1:T(2,128)(2,1)} copy(bf16[1,2152,512]{2,1,0:T(8,128)(2,1)S(1)} %fusion.33) | data formatting | bytes 4407296 | tf_op jit(solution)/shard_map/convert_element_type | solution.py:218
  610.1 16.1 %reduce.1 = bf16[2152,512]{1,0:T(8,128)(2,1)} reduce(bf16[2152,1,512]{2,1,0:T(2,128)(2,1)} %bitcast.161, bf16[]{:T(256)} %broadcast.495), dimensions={1}, to_apply=%bitcast.152.reduce_sub_computation | reduce | bytes 4407298
  637.0 9.8 fusion.35
  646.9 9.9 fusion.34
  656.8 26.4 %all-to-all-done.3 = bf16[8,2,68864]{2,1,0:T(2,128)(2,1)} async-done(((bf16[8,2,68864]{2,1,0:T(2,128)(2,1)}), bf16[8,2,68864]{2,1,0:T(2,128)(2,1)}, u32[]{:S(2)}, u32[]{:S(2)}) %all-to-all-start.3) | async-done | bytes 2203680 | tf_op jit(solution)/shard_map/all_to_all | solution.py:219
  765.7 12.3 %reduce-scatter.10.cloned.1.call-done = f32[16,8]{1,0:T(8,128)} async-done(((f32[512,8]{1,0:T(8,128)}), f32[16,8]{1,0:T(8,128)}) %reduce-scatter.10.cloned.1.call-update) | async-done | bytes 528
  779.4 85.5 %all-reduce.11.cloned.1.call-done = (bf16[1,512,2048]{2,1,0:T(8,128)(2,1)}, bf16[1,2048,512]{2,1,0:T(8,128)(2,1)}) async-done(((bf16[1,512,2048]{2,1,0:T(8,128)(2,1)}, bf16[1,2048,512]{2,1,0:T(8,128)(2,1)}), (bf16[1,512,2048]{2,1,0:T(8,128)(2,1)}, bf16[1,2048,512]{2,1,0:T(8,128)(2,1)})) %all-reduce.11.cloned.1.call-update) | async-done | bytes 4194320 | tf_op jit(solution)/shard_map/psum | solution.py:264
  876.5 39.7 %all-reduce.6 = (f32[512]{0:T(512)S(1)}, f32[512]{0:T(512)S(1)}) all-reduce(f32[512]{0:T(512)S(1)} %get-tuple-element.47, f32[512]{0:T(512)S(1)} %get-tuple-element.45), channel_id=2, replica_groups=mesh['grp'=4,'ep'=8] {'grp','ep'}, use_global_device_ids=true, to_apply=%region_29.30.clone | all-reduce | flops 1024 | bytes 8192
  925.9 77.0 %reduce-scatter.8.cloned.1.call-done = f32[16,512]{1,0:T(8,128)} async-done(((f32[512,512]{1,0:T(8,128)}), f32[16,512]{1,0:T(8,128)}) %reduce-scatter.8.cloned.1.call-update) | async-done | bytes 32784 | tf_op jit(solution)/shard_map/reduce_scatter | solution.py:259
  1002.9 104.5 %reduce-scatter.6.cloned.1.call-done = f32[16,1536]{1,0:T(8,128)} async-done(((f32[512,1536]{1,0:T(8,128)}), f32[16,1536]{1,0:T(8,128)}) %reduce-scatter.6.cloned.1.call-update) | async-done | bytes 98320 | tf_op jit(solution)/shard_map/reduce_scatter | solution.py:258
  (269 shorter events, 240.5 us)
Async XLA Ops:
  7.2 249.5 %copy-start = (bf16[1,512,2048]{2,1,0:T(8,128)(2,1)S(1)}, bf16[1,512,2048]{2,1,0:T(8,128)(2,1)}, u32[]{:S(2)}) copy-start(bf16[1,512,2048]{2,1,0:T(8,128)(2,1)} %param.23) | copy-start | bytes 6291460
  7.2 57.0 %copy-start.46 = (s32[1024,2]{0,1:T(2,128)S(1)}, s32[1024,2]{0,1:T(2,128)}, u32[]{:S(2)}) copy-start(s32[1024,2]{0,1:T(2,128)} %param.16) | copy-start | bytes 24580
  7.2 58.4 %copy-start.51 = (bf16[16,512]{1,0:T(8,128)(2,1)S(1)}, bf16[16,512]{1,0:T(8,128)(2,1)}, u32[]{:S(2)}) copy-start(bf16[16,512]{1,0:T(8,128)(2,1)} %param.20) | copy-start | bytes 49156
  7.2 132.5 %all-gather.3.cloned.1.call-start = ((), (), s32[]{:S(2)}) async-start(), calls=%async_computation.7 | async-start | bytes 1622016 | tf_op jit(solution)/shard_map/all_gather | solution.py:135
  9.5 159.7 %copy-start.7 = (bf16[1024,512]{0,1:T(8,128)(2,1)}, bf16[1024,512]{0,1:T(8,128)(2,1)S(1)}, u32[]{:S(2)}) copy-start(bf16[1024,512]{0,1:T(8,128)(2,1)S(1)} %copy.92) | copy-start | bytes 3145732
  53.3 89.8 %copy-start.58 = (f32[512]{0:T(512)}, f32[512]{0:T(512)S(1)}, u32[]{:S(2)}) copy-start(f32[512]{0:T(512)S(1)} %convert_element_type.142) | copy-start | bytes 6148
  54.8 115.5 %copy-start.47 = (f32[512]{0:T(512)}, f32[512]{0:T(512)S(1)}, u32[]{:S(2)}) copy-start(f32[512]{0:T(512)S(1)} %convert_element_type.148) | copy-start | bytes 6148
  63.8 79.3 %copy-start.40 = (f32[1024]{0:T(1024)}, f32[1024]{0:T(1024)S(1)}, u32[]{:S(2)}) copy-start(f32[1024]{0:T(1024)S(1)} %broadcast_multiply_fusion.5) | copy-start | bytes 12292
  64.1 79.0 %copy-start.49 = (f32[1024]{0:T(1024)}, f32[1024]{0:T(1024)S(1)}, u32[]{:S(2)}) copy-start(f32[1024]{0:T(1024)S(1)} %add_rsqrt_fusion.1) | copy-start | bytes 12292
  64.2 109.2 %copy-start.52 = (s32[1024,1]{0,1:T(1,128)}, s32[1024,1]{0,1:T(1,128)S(1)}, u32[]{:S(2)}) copy-start(s32[1024,1]{0,1:T(1,128)S(1)} %get-tuple-element.73) | copy-start | bytes 12292
  172.1 21.1 %copy-start.9 = (bf16[1024,512]{0,1:T(8,128)(2,1)}, bf16[1024,512]{0,1:T(8,128)(2,1)S(1)}, u32[]{:S(2)}) copy-start(bf16[1024,512]{0,1:T(8,128)(2,1)S(1)} %multiply_convert_fusion.2) | copy-start | bytes 3145732
  256.7 43.5 %copy-start.61 = (bf16[1,2048,512]{2,1,0:T(8,128)(2,1)S(1)}, bf16[1,2048,512]{2,1,0:T(8,128)(2,1)}, u32[]{:S(2)}) copy-start(bf16[1,2048,512]{2,1,0:T(8,128)(2,1)} %param.24) | copy-start | bytes 6291460
  343.2 108.5 %copy-start.53 = (s32[1024,1]{0,1:T(1,128)S(1)}, s32[1024,1]{0,1:T(1,128)}, u32[]{:S(2)}) copy-start(s32[1024,1]{0,1:T(1,128)} %copy-done.52) | copy-start | bytes 12292
  343.2 108.6 %copy-start.43 = (s32[1,2,4,128]{3,1,2,0:T(2,128)S(1)}, s32[1,2,4,128]{3,1,2,0:T(2,128)}, u32[]{:S(2)}) copy-start(s32[1,2,4,128]{3,1,2,0:T(2,128)} %copy-done.42) | copy-start | bytes 12292
  343.2 108.6 %copy-start.55 = (s32[1024]{0:T(1024)S(1)}, s32[1024]{0:T(1024)}, u32[]{:S(2)}) copy-start(s32[1024]{0:T(1024)} %copy-done.54) | copy-start | bytes 12292
  343.2 108.6 %copy-start.57 = (s32[1024]{0:T(1024)S(1)}, s32[1024]{0:T(1024)}, u32[]{:S(2)}) copy-start(s32[1024]{0:T(1024)} %copy-done.56) | copy-start | bytes 12292
  343.2 110.1 %all-to-all-start.1 = ((bf16[8,2,68864]{2,1,0:T(2,128)(2,1)}), bf16[8,2,68864]{2,1,0:T(2,128)(2,1)}, u32[]{:S(2)}, u32[]{:S(2)}) async-start(bf16[8,2,68864]{2,1,0:T(2,128)(2,1)} %reshape.505), calls=%async_computation.1 | async-start | bytes 4407296 | tf_op jit(solution)/shard_map/all_to_all | solution.py:182
  630.1 53.2 %all-to-all-start.3 = ((bf16[8,2,68864]{2,1,0:T(2,128)(2,1)}), bf16[8,2,68864]{2,1,0:T(2,128)(2,1)}, u32[]{:S(2)}, u32[]{:S(2)}) async-start(bf16[8,2,68864]{2,1,0:T(2,128)(2,1)} %reshape.507), calls=%async_computation.3 | async-start | bytes 4407296 | tf_op jit(solution)/shard_map/all_to_all | solution.py:219
  634.5 143.6 %reduce-scatter.10.cloned.1.call-start = ((), (), s32[]{:S(2)}) async-start(), calls=%async_computation.10 | async-start | bytes 270336
  637.0 227.9 %all-reduce.11.cloned.1.call-start = ((), (), s32[]{:S(2)}) async-start(), calls=%async_computation.11 | async-start | bytes 8388608 | tf_op jit(solution)/shard_map/psum | solution.py:264
  637.0 9.8 copy-start.20
  656.8 346.1 %reduce-scatter.8.cloned.1.call-start = ((), (), s32[]{:S(2)}) async-start(), calls=%async_computation.9 | async-start | bytes 1081344 | tf_op jit(solution)/shard_map/reduce_scatter | solution.py:259
  720.0 11.2 %copy-start.6 = (f32[1024,512]{0,1:T(8,128)}, f32[1024,512]{0,1:T(8,128)S(1)}, u32[]{:S(2)}) copy-start(f32[1024,512]{0,1:T(8,128)S(1)} %get-tuple-element.66) | copy-start | bytes 6291460
  746.4 361.0 %reduce-scatter.6.cloned.1.call-start = ((), (), s32[]{:S(2)}) async-start(), calls=%async_computation.8 | async-start | bytes 3244032 | tf_op jit(solution)/shard_map/reduce_scatter | solution.py:258
  (52 other events, 211.4 us)
Sparse Core Ops, SparseCore 0:
  10.9 57.7 all-gather.2
  637.5 140.4 reduce-scatter.9
  781.2 83.6 all-reduce.10
  867.6 135.2 reduce-scatter.7
  1009.6 97.7 reduce-scatter.5
where the time goes:
time: 1120 us; the launch traced here: 1110 us
  blocking collectives  363 us (32%)
  waiting for transfers between devices  307 us (27%)
  local copies, waits for them, and re-layouts  164 us (15%)
  matrix products  154 us (14%)
  other arithmetic  102 us (9%)
  between operations  15 us (1%)
    reduce_scatter x1, waiting for transfers between devices, per_device(): lax.psum_scatter(grad_joint_w, ('grp', 'ep'), scatter_dimension=0, tiled=...  105 us
    all_gather x1, blocking collectives, per_device(): lax.all_gather(router_weight, ('grp', 'ep'), axis=0, tiled=True)  102 us
    psum x1, waiting for transfers between devices, per_device(): lax.psum(grad_up.astype(jnp.bfloat16), 'grp').astype(jnp.float32)  85.5 us
    unnamed x2, blocking collectives  81.8 us
    reduce_scatter x1, waiting for transfers between devices, per_device(): lax.psum_scatter(grad_output_w, ('grp', 'ep'), scatter_dimension=0, tiled...  77 us
    all_gather x1, blocking collectives, per_device(): lax.all_gather(output_weight, ('grp', 'ep'), axis=0, tiled=True)  74.1 us
    unnamed x160, local copies, waits for them, and re-layouts  56.1 us
    all_to_all x1, blocking collectives, per_device(): lax.all_to_all(outgoing, 'ep', split_axis=0, concat_axis=1, tiled=True)  53 us
  transfers between devices with their start and end apart: 7, of which 5 were waited for; matrix products, arithmetic and copies ran while one was open for 12% of the time, Pallas kernels for 0%

commit v1 on v0

--- a/solution.py
+++ b/solution.py
@@ -6,6 +6,19 @@
 HEADS = 8
 EPSILON = 1e-06
 NEGATIVE = -1e30
+
+
+def _prepare_spot(x_local, k_dim, my_tile):
+    ready, base_arr = (x_local.shape[:k_dim], x_local.shape[k_dim + 1 :])
+    parts_out = jnp.moveaxis(x_local.reshape(*ready, my_tile, -1, *base_arr), k_dim, 0)
+    return parts_out
+
+
+def note_members_all(xx, d_out):
+    xx = jnp.moveaxis(xx, 0, d_out)
+    mat_out = xx.shape
+    y2 = xx.reshape(*mat_out[:d_out], mat_out[d_out] * mat_out[d_out + 1], *mat_out[d_out + 2 :])
+    return y2
 
 
 def normalize(values, gain):
@@ -216,7 +229,16 @@
     grad_rows = jnp.einsum(
         "erf,edf->erd", grad_pre, expert_up, preferred_element_type=jnp.float32
     ).astype(jnp.bfloat16)
-    grad_back = lax.all_to_all(grad_rows, "ep", split_axis=1, concat_axis=0, tiled=True)
+    d_next, block_now = (lax.axis_size("ep"), lax.axis_index("ep"))
+    mid_arr = _prepare_spot(grad_rows, 1, d_next)
+    chunks = [mid_arr[block_now]]
+    for i0 in tuple(range(1, d_next)):
+        state_now = mid_arr[(block_now + i0) % d_next]
+        chunks.append(
+            lax.ppermute(state_now, "ep", perm=[(rr, (rr + i0) % d_next) for rr in range(d_next)])
+        )
+    mid_arr = jnp.stack(chunks, axis=0)[(block_now - jnp.arange(d_next)) % d_next]
+    grad_back = note_members_all(mid_arr, 0)
     flat_grad = jnp.concatenate(
         [grad_back.reshape(expert_count * capacity, width), zero_row], axis=0
     )

time: 1120 us -> 1020 us (0.911)
  waiting for transfers between devices: 307 us -> 245 us
  blocking collectives: 363 us -> 328 us
  other arithmetic: 102 us -> 85.8 us
    psum x1, waiting for transfers between devices: 85.5 us -> 0.01 us  [per_device(): lax.psum(grad_up.astype(jnp.bfloat16), 'grp').astype(jnp.float32)]
    all_to_all x1 -> x0, blocking collectives: 52 us -> none  [per_device(): lax.all_to_all(grad_out_rows, 'ep', split_axis=0, concat_axis=1, tiled=True)]
    all_to_all x1, waiting for transfers between devices: 26.4 us -> 45.2 us  [per_device(): lax.all_to_all(grad_out_rows, 'ep', split_axis=0, concat_axis=1, tiled=True)]
    convert_element_type x1 -> x0, local copies, waits for them, and re-layouts: 16.4 us -> none  [per_device(): grad_rows = jnp.einsum('erf,edf->erd', grad_pre, expert_up, preferred_ele...]
    unnamed x2, blocking collectives: 81.8 us -> 98.2 us
    unnamed x5 -> x4, other arithmetic: 33.3 us -> 16.9 us
    ppermute x0 -> x7, waiting for transfers between devices: none -> 13.2 us  [per_device(): lax.ppermute(state_now, 'ep', perm=[(rr, (rr + i0) % d_next) for rr in ra...]
    unnamed x6, waiting for transfers between devices: 13.1 us -> 0.77 us
  transfers between devices with their start and end apart: 7 -> 14, of which waited for: 5 -> 5; matrix products, arithmetic and copies ran while one was open for 12% -> 17% of each run, Pallas kernels for 0% -> 0%
where the time goes in v1:
time: 1020 us; the launch traced here: 1010 us
  blocking collectives  328 us (32%)
  waiting for transfers between devices  245 us (24%)
  local copies, waits for them, and re-layouts  161 us (16%)
  matrix products  156 us (15%)
  other arithmetic  85.8 us (8%)
  starting transfers between devices  19.2 us (2%)
  between operations  15.1 us (1%)
    reduce_scatter x1, waiting for transfers between devices, per_device(): lax.psum_scatter(grad_joint_w, ('grp', 'ep'), scatter_dimension=0, tiled=...  104 us
    all_gather x1, blocking collectives, per_device(): lax.all_gather(router_weight, ('grp', 'ep'), axis=0, tiled=True)  102 us
    unnamed x2, blocking collectives  98.2 us
    reduce_scatter x1, waiting for transfers between devices, per_device(): lax.psum_scatter(grad_output_w, ('grp', 'ep'), scatter_dimension=0, tiled...  81.1 us
    all_gather x1, blocking collectives, per_device(): lax.all_gather(output_weight, ('grp', 'ep'), axis=0, tiled=True)  73.9 us
    all_to_all x1, blocking collectives, per_device(): lax.all_to_all(outgoing, 'ep', split_axis=0, concat_axis=1, tiled=True)  53.3 us
    unnamed x165, local copies, waits for them, and re-layouts  53 us
    all_to_all x1, waiting for transfers between devices, per_device(): lax.all_to_all(grad_out_rows, 'ep', split_axis=0, concat_axis=1, tiled=True)  45.2 us
  transfers between devices with their start and end apart: 14, of which 5 were waited for; matrix products, arithmetic and copies ran while one was open for 17% of the time, Pallas kernels for 0%

profile of v1, /device:TPU:0, one launch (start us, length us, event | category | flops | bytes accessed | tf_op | source)
XLA Modules:
  0.0 1009.2 jit_solution(15393945243241107567)
XLA Ops:
  11.2 42.1 %all-reduce.7 = (bf16[512]{0:T(512)(128)(2,1)S(1)}, bf16[512]{0:T(512)(128)(2,1)S(1)}) all-reduce(bf16[512]{0:T(512)(128)(2,1)S(1)} %dynamic-update-slice, bf16[512]{0:T(512)(128)(2,1)S(1)} %dynamic-update-slice.1), channel_id=1, replica_groups=mesh['grp'=4,'ep'=8] {'grp','ep'}, use_global_device_ids=true, to_apply=%add.2 | all-reduce | flops 1024 | bytes 4096
  64.9 73.9 %all_gather.17 = bf16[512,512]{1,0:T(8,128)(2,1)} all-gather(bf16[16,512]{1,0:T(8,128)(2,1)S(1)} %copy-done.51), channel_id=1, replica_groups=mesh['grp'=4,'ep'=8] {'grp','ep'}, dimensions={0}, use_global_device_ids=true | all-gather | bytes 540672 | tf_op jit(solution)/shard_map/all_gather | solution.py:149
  172.1 9.2 scatter_custom_fusion
  181.3 10.6 %scatter_fusion = bf16[2153,512]{1,0:T(8,128)(2,1)} fusion(bf16[2153,512]{1,0:T(8,128)(2,1)} %scatter_custom_fusion, s32[1024]{0:T(1024)S(1)} %bitcast.202, bf16[1024,512]{1,0:T(8,128)(2,1)} %copy.97), kind=kCustom, calls=%fused_computation.6 | custom fusion | flops 524288 | bytes 3149824 | tf_op jit(solution)/shard_map/scatter-add | solution.py:187
  198.7 53.3 %all_to_all.12 = bf16[8,269,512]{2,1,0:T(8,128)(2,1)} all-to-all(bf16[8,269,512]{2,1,0:T(8,128)(2,1)} %reshape.464), channel_id=1, replica_groups=mesh['grp'=4,'ep'=8] {'ep'}, dimensions={0} | all-to-all | bytes 4407296 | tf_op jit(solution)/shard_map/all_to_all | solution.py:189
  255.7 43.6 %fusion.2 = (bf16[2152,2048]{1,0:T(8,128)(2,1)S(1)}, f32[2152,2048]{1,0:T(8,128)}) fusion(bf16[2152,512]{1,0:T(8,128)(2,1)} %reshape.465, bf16[1,512,2048]{2,1,0:T(8,128)(2,1)S(1)} %copy-done), kind=kOutput, calls=%fused_computation.13 | convolution fusion | flops 4799545344 | bytes 30744576 | tf_op jit(solution)/shard_map/erd,edf->erf/dot_general | solution.py:190
  305.0 16.5 %copy.132 = bf16[1,2152,512]{2,0,1:T(2,128)(2,1)} copy(bf16[1,2152,512]{2,1,0:T(8,128)(2,1)S(1)} %fusion.32) | data formatting | bytes 4407296 | tf_op jit(solution)/shard_map/convert_element_type | solution.py:194
  322.0 16.2 %reduce = bf16[2152,512]{1,0:T(8,128)(2,1)} reduce(bf16[2152,1,512]{2,1,0:T(2,128)(2,1)} %bitcast.181, bf16[]{:T(256)} %broadcast.575), dimensions={1}, to_apply=%bitcast.175.reduce_sub_computation | reduce | bytes 4407298
  347.9 102.5 %all-gather = bf16[32,16,8]{1,2,0:T(8,128)(2,1)S(1)} all-gather(bf16[1,16,8]{1,2,0:T(8,128)(2,1)S(1)} %bitcast.225), channel_id=1, replica_groups=mesh['grp'=4,'ep'=8] {'grp','ep'}, dimensions={0}, use_global_device_ids=true | all-gather | bytes 8448 | tf_op jit(solution)/shard_map/all_gather | solution.py:151
  452.2 7.9 reshape.559
  464.5 7.0 gather_fusion.1
  473.8 7.0 gather_fusion
  491.7 9.0 scatter_custom_fusion.2
  500.7 11.0 %scatter_fusion.1 = bf16[2153,512]{1,0:T(8,128)(2,1)} fusion(bf16[2153,512]{1,0:T(8,128)(2,1)} %scatter_custom_fusion.2, s32[1024]{0:T(1024)S(1)} %bitcast.204, bf16[1024,512]{1,0:T(8,128)(2,1)} %copy.104), kind=kCustom, calls=%fused_computation.8 | custom fusion | flops 524288 | bytes 3149824 | tf_op jit(solution)/shard_map/scatter-add | solution.py:215
  525.7 45.2 %all-to-all-done.2 = bf16[8,269,512]{2,1,0:T(8,128)(2,1)} async-done(((bf16[8,269,512]{2,1,0:T(8,128)(2,1)}), bf16[8,269,512]{2,1,0:T(8,128)(2,1)}, u32[]{:S(2)}, u32[]{:S(2)}) %all-to-all-start.2) | async-done | bytes 2203680 | tf_op jit(solution)/shard_map/all_to_all | solution.py:217
  574.6 9.3 fusion.34
  583.9 12.4 %fusion.8 = bf16[2152,2048]{1,0:T(8,128)(2,1)S(1)} fusion(f32[2152,2048]{1,0:T(8,128)} %get-tuple-element.95, bf16[2152,512]{1,0:T(8,128)(2,1)S(1)} %copy-done.20, bf16[1,2048,512]{2,1,0:T(8,128)(2,1)S(1)} %copy-done.62), kind=kOutput, calls=%fused_computation.19 | convolution fusion | flops 4557144064 | bytes 30744576 | tf_op jit(solution)/shard_map/erd,efd->erf/dot_general | solution.py:224
  614.0 9.9 fusion.33
  635.9 10.8 %collective-permute-done.2 = bf16[1,269,512]{2,1,0:T(8,128)(2,1)} collective-permute-done((bf16[1,269,512]{2,1,0:T(8,128)(2,1)}, bf16[1,269,512]{2,1,0:T(8,128)(2,1)}, u32[]{:S(2)}, u32[]{:S(2)}) %collective-permute-start.2) | collective-permute-done | bytes 275488 | tf_op jit(solution)/shard_map/ppermute | solution.py:238
  666.0 7.0 gather_fusion.3
  673.1 7.0 gather_fusion.4
  744.3 56.1 %all-reduce.6 = (f32[512]{0:T(512)S(1)}, f32[512]{0:T(512)S(1)}) all-reduce(f32[512]{0:T(512)S(1)} %get-tuple-element.47, f32[512]{0:T(512)S(1)} %get-tuple-element.45), channel_id=2, replica_groups=mesh['grp'=4,'ep'=8] {'grp','ep'}, use_global_device_ids=true, to_apply=%region_29.30.clone | all-reduce | flops 1024 | bytes 8192
  816.9 81.1 %reduce-scatter.8.cloned.1.call-done = f32[16,512]{1,0:T(8,128)} async-done(((f32[512,512]{1,0:T(8,128)}), f32[16,512]{1,0:T(8,128)}) %reduce-scatter.8.cloned.1.call-update) | async-done | bytes 32784 | tf_op jit(solution)/shard_map/reduce_scatter | solution.py:281
  898.0 104.5 %reduce-scatter.6.cloned.1.call-done = f32[16,1536]{1,0:T(8,128)} async-done(((f32[512,1536]{1,0:T(8,128)}), f32[16,1536]{1,0:T(8,128)}) %reduce-scatter.6.cloned.1.call-update) | async-done | bytes 98320 | tf_op jit(solution)/shard_map/reduce_scatter | solution.py:280
  (291 shorter events, 240.8 us)
Async XLA Ops:
  7.2 248.5 %copy-start = (bf16[1,512,2048]{2,1,0:T(8,128)(2,1)S(1)}, bf16[1,512,2048]{2,1,0:T(8,128)(2,1)}, u32[]{:S(2)}) copy-start(bf16[1,512,2048]{2,1,0:T(8,128)(2,1)} %param.23) | copy-start | bytes 6291460
  7.2 131.6 %all-gather.3.cloned.1.call-start = ((), (), s32[]{:S(2)}) async-start(), calls=%async_computation.6 | async-start | bytes 1622016 | tf_op jit(solution)/shard_map/all_gather | solution.py:148
  9.5 158.3 %copy-start.7 = (bf16[1024,512]{0,1:T(8,128)(2,1)}, bf16[1024,512]{0,1:T(8,128)(2,1)S(1)}, u32[]{:S(2)}) copy-start(bf16[1024,512]{0,1:T(8,128)(2,1)S(1)} %copy.91) | copy-start | bytes 3145732
  53.3 88.8 %copy-start.58 = (f32[512]{0:T(512)}, f32[512]{0:T(512)S(1)}, u32[]{:S(2)}) copy-start(f32[512]{0:T(512)S(1)} %convert_element_type.140) | copy-start | bytes 6148
  54.8 114.1 %copy-start.47 = (f32[512]{0:T(512)}, f32[512]{0:T(512)S(1)}, u32[]{:S(2)}) copy-start(f32[512]{0:T(512)S(1)} %convert_element_type.146) | copy-start | bytes 6148
  63.1 79.1 %copy-start.40 = (f32[1024]{0:T(1024)}, f32[1024]{0:T(1024)S(1)}, u32[]{:S(2)}) copy-start(f32[1024]{0:T(1024)S(1)} %broadcast_multiply_fusion.5) | copy-start | bytes 12292
  63.5 108.6 %copy-start.56 = (s32[1024,1]{0,1:T(1,128)}, s32[1024,1]{0,1:T(1,128)S(1)}, u32[]{:S(2)}) copy-start(s32[1024,1]{0,1:T(1,128)S(1)} %get-tuple-element.81) | copy-start | bytes 12292
  342.0 108.5 %copy-start.43 = (s32[1,2,4,128]{3,1,2,0:T(2,128)S(1)}, s32[1,2,4,128]{3,1,2,0:T(2,128)}, u32[]{:S(2)}) copy-start(s32[1,2,4,128]{3,1,2,0:T(2,128)} %copy-done.42) | copy-start | bytes 12292
  342.0 108.5 %copy-start.53 = (s32[1024]{0:T(1024)S(1)}, s32[1024]{0:T(1024)}, u32[]{:S(2)}) copy-start(s32[1024]{0:T(1024)} %copy-done.52) | copy-start | bytes 12292
  342.0 108.6 %copy-start.55 = (s32[1024]{0:T(1024)S(1)}, s32[1024]{0:T(1024)}, u32[]{:S(2)}) copy-start(s32[1024]{0:T(1024)} %copy-done.54) | copy-start | bytes 12292
  342.0 108.6 %copy-start.57 = (s32[1024,1]{0,1:T(1,128)S(1)}, s32[1024,1]{0,1:T(1,128)}, u32[]{:S(2)}) copy-start(s32[1024,1]{0,1:T(1,128)} %copy-done.56) | copy-start | bytes 12292
  342.0 110.1 %all-to-all-start.1 = ((bf16[8,2,68864]{2,1,0:T(2,128)(2,1)}), bf16[8,2,68864]{2,1,0:T(2,128)(2,1)}, u32[]{:S(2)}, u32[]{:S(2)}) async-start(bf16[8,2,68864]{2,1,0:T(2,128)(2,1)} %reshape.558), calls=%async_computation.1 | async-start | bytes 4407296 | tf_op jit(solution)/shard_map/all_to_all | solution.py:195
  518.5 52.4 %all-to-all-start.2 = ((bf16[8,269,512]{2,1,0:T(8,128)(2,1)}), bf16[8,269,512]{2,1,0:T(8,128)(2,1)}, u32[]{:S(2)}, u32[]{:S(2)}) async-start(bf16[8,269,512]{2,1,0:T(8,128)(2,1)} %reshape.469), calls=%async_computation.2 | async-start | bytes 4456448 | tf_op jit(solution)/shard_map/all_to_all | solution.py:217
  523.0 214.1 %reduce-scatter.10.cloned.1.call-start = ((), (), s32[]{:S(2)}) async-start(), calls=%async_computation.9 | async-start | bytes 270336
  525.6 284.4 %all-reduce.11.cloned.1.call-start = ((), (), s32[]{:S(2)}) async-start(), calls=%async_computation.10 | async-start | bytes 8388608 | tf_op jit(solution)/shard_map/psum | solution.py:286
  612.6 17.3 %collective-permute-start = (bf16[1,269,512]{2,1,0:T(8,128)(2,1)}, bf16[1,269,512]{2,1,0:T(8,128)(2,1)}, u32[]{:S(2)}, u32[]{:S(2)}) collective-permute-start(bf16[1,269,512]{2,1,0:T(8,128)(2,1)} %get-tuple-element.72), channel_id=1, source_target_pairs={{0,1},{1,2},{2,3},{3,4},{4,5},{5,6},{6,7},{7,0},{8,9},{9,10},{10,1... | collective-permute-start | bytes 826376 | tf_op jit(solution)/shard_map/ppermute | solution.py:238
  613.9 19.5 %collective-permute-start.1 = (bf16[1,269,512]{2,1,0:T(8,128)(2,1)}, bf16[1,269,512]{2,1,0:T(8,128)(2,1)}, u32[]{:S(2)}, u32[]{:S(2)}) collective-permute-start(bf16[1,269,512]{2,1,0:T(8,128)(2,1)} %get-tuple-element.71), channel_id=1, source_target_pairs={{0,2},{1,3},{2,4},{3,5},{4,6},{5,7},{6,0},{7,1},{8,10},{9,11},{10,... | collective-permute-start | bytes 826376 | tf_op jit(solution)/shard_map/ppermute | solution.py:238
  624.0 22.7 %collective-permute-start.2 = (bf16[1,269,512]{2,1,0:T(8,128)(2,1)}, bf16[1,269,512]{2,1,0:T(8,128)(2,1)}, u32[]{:S(2)}, u32[]{:S(2)}) collective-permute-start(bf16[1,269,512]{2,1,0:T(8,128)(2,1)} %get-tuple-element.70), channel_id=1, source_target_pairs={{0,3},{1,4},{2,5},{3,6},{4,7},{5,0},{6,1},{7,2},{8,11},{9,12},{10,... | collective-permute-start | bytes 826376 | tf_op jit(solution)/shard_map/ppermute | solution.py:238
  626.2 24.5 %collective-permute-start.3 = (bf16[1,269,512]{2,1,0:T(8,128)(2,1)}, bf16[1,269,512]{2,1,0:T(8,128)(2,1)}, u32[]{:S(2)}, u32[]{:S(2)}) collective-permute-start(bf16[1,269,512]{2,1,0:T(8,128)(2,1)} %get-tuple-element.69), channel_id=1, source_target_pairs={{0,4},{1,5},{2,6},{3,7},{4,0},{5,1},{6,2},{7,3},{8,12},{9,13},{10,... | collective-permute-start | bytes 826376 | tf_op jit(solution)/shard_map/ppermute | solution.py:238
  628.0 24.4 %collective-permute-start.4 = (bf16[1,269,512]{2,1,0:T(8,128)(2,1)}, bf16[1,269,512]{2,1,0:T(8,128)(2,1)}, u32[]{:S(2)}, u32[]{:S(2)}) collective-permute-start(bf16[1,269,512]{2,1,0:T(8,128)(2,1)} %get-tuple-element.68), channel_id=1, source_target_pairs={{0,5},{1,6},{2,7},{3,0},{4,1},{5,2},{6,3},{7,4},{8,13},{9,14},{10,... | collective-permute-start | bytes 826376 | tf_op jit(solution)/shard_map/ppermute | solution.py:238
  629.8 268.2 %reduce-scatter.8.cloned.1.call-start = ((), (), s32[]{:S(2)}) async-start(), calls=%async_computation.8 | async-start | bytes 1081344 | tf_op jit(solution)/shard_map/reduce_scatter | solution.py:281
  629.9 24.2 %collective-permute-start.5 = (bf16[1,269,512]{2,1,0:T(8,128)(2,1)}, bf16[1,269,512]{2,1,0:T(8,128)(2,1)S(1)}, u32[]{:S(2)}, u32[]{:S(2)}) collective-permute-start(bf16[1,269,512]{2,1,0:T(8,128)(2,1)} %get-tuple-element.67), channel_id=1, source_target_pairs={{0,6},{1,7},{2,0},{3,1},{4,2},{5,3},{6,4},{7,5},{8,14},{9,15},{10,... | collective-permute-start | bytes 826376 | tf_op jit(solution)/shard_map/ppermute | solution.py:238
  633.4 21.5 %collective-permute-start.6 = (bf16[1,269,512]{2,1,0:T(8,128)(2,1)S(1)}, bf16[1,269,512]{2,1,0:T(8,128)(2,1)S(1)}, u32[]{:S(2)}, u32[]{:S(2)}) collective-permute-start(bf16[1,269,512]{2,1,0:T(8,128)(2,1)S(1)} %get-tuple-element.66), channel_id=1, source_target_pairs={{0,7},{1,0},{2,1},{3,2},{4,3},{5,4},{6,5},{7,6},{8,15},{9,8},{10,9... | collective-permute-start | bytes 826376 | tf_op jit(solution)/shard_map/ppermute | solution.py:238
  717.0 285.4 %reduce-scatter.6.cloned.1.call-start = ((), (), s32[]{:S(2)}) async-start(), calls=%async_computation.7 | async-start | bytes 3244032 | tf_op jit(solution)/shard_map/reduce_scatter | solution.py:280
  (60 other events, 527.9 us)
Sparse Core Ops, SparseCore 0:
  10.9 57.8 all-gather.2
  526.1 147.3 reduce-scatter.9
  676.1 83.8 all-reduce.10
  762.7 135.2 reduce-scatter.7
  904.7 97.6 reduce-scatter.5
